TPU v7x, 32 devices: a whole 2x2x4 slice. The times are simulated.
32 devices in a mesh: fsdp: 8 (over z, y), tp: 4 (over x, core).
Axes of the slice: x: 2, y: 2, z: 4, core: 2. Of those that a mesh axis runs over, the one named last changes fastest.
Arguments:
- inputs: bfloat16 [16, 736, 1152], P('fsdp', 'tp'), may hold values from -6 to 6
- cotangent: bfloat16 [16, 736, 1152], P('fsdp', 'tp'), may hold values from -6 to 6
- lengths: int32 [16], P('fsdp'), may hold values from 1 to 729, as said below
- ln1_gain: bfloat16 [1152], P('fsdp'), may hold values from 0.099609375 to 1.8984375
- ln1_bias: bfloat16 [1152], P('fsdp'), may hold values from -0.3125 to 0.3125
- q_weight: bfloat16 [1152, 1152], P('fsdp', 'tp'), may hold values from -0.1875 to 0.1875
- q_bias: bfloat16 [1152], P('tp'), may hold values from -3 to 3
- k_weight: bfloat16 [1152, 1152], P('fsdp', 'tp'), may hold values from -0.1875 to 0.1875
- v_weight: bfloat16 [1152, 1152], P('fsdp', 'tp'), may hold values from -0.1875 to 0.1875
- v_bias: bfloat16 [1152], P('tp'), may hold values from -0.1875 to 0.1875
- out_weight: bfloat16 [1152, 1152], P('tp', 'fsdp'), may hold values from -2.5 to 2.5
- out_bias: bfloat16 [1152], P('fsdp'), may hold values from -1.75 to 1.75
- ln2_gain: bfloat16 [1152], P('fsdp'), may hold values from 0.099609375 to 1.8984375
- ln2_bias: bfloat16 [1152], P('fsdp'), may hold values from -1.75 to 1.75
- up_weight: bfloat16 [1152, 4304], P('fsdp', 'tp'), may hold values from -0.1875 to 0.1875
- up_bias: bfloat16 [4304], P('tp'), may hold values from -1.75 to 1.75
- down_weight: bfloat16 [4304, 1152], P('tp', 'fsdp'), may hold values from -0.09375 to 0.09375
- down_bias: bfloat16 [1152], P('fsdp'), may hold values from -1.75 to 1.75
Outputs:
- layer_out: bfloat16 [16, 736, 1152], P('fsdp', 'tp')
- input_grad: float32 [16, 736, 1152], P('fsdp', 'tp')
- ln1_gain_grad: float32 [1152], P('fsdp')
- ln1_bias_grad: float32 [1152], P('fsdp')
- q_weight_grad: float32 [1152, 1152], P('fsdp', 'tp')
- q_bias_grad: float32 [1152], P('tp')
- k_weight_grad: float32 [1152, 1152], P('fsdp', 'tp')
- v_weight_grad: float32 [1152, 1152], P('fsdp', 'tp')
- v_bias_grad: float32 [1152], P('tp')
- out_weight_grad: float32 [1152, 1152], P('tp', 'fsdp')
- out_bias_grad: float32 [1152], P('fsdp')
- ln2_gain_grad: float32 [1152], P('fsdp')
- ln2_bias_grad: float32 [1152], P('fsdp')
- up_weight_grad: float32 [1152, 4304], P('fsdp', 'tp')
- up_bias_grad: float32 [4304], P('tp')
- down_weight_grad: float32 [4304, 1152], P('tp', 'fsdp')
- down_bias_grad: float32 [1152], P('fsdp')
Inputs may be any that keep to these rules, and one draw needn't show every extreme that they name: `lengths`: each slot either holds one image of 729 tokens or is empty with length 1; exactly 11 slots hold images, which ones drawn from the seed.
All inputs are finite; a program needn't handle non-finite values.
Results may differ from a plain program's by a relative error of at most 0.013.
Values may be sent and summed in bfloat16 or wider, within the bound.
No kernel may reach another device: no remote copies, remote signals or barrier semaphores. Data moves between devices by JAX's collectives and lax.ppermute only.
A program may use at most 192 MiB of HBM per device.

v0:
```python
import jax
import jax.numpy as jnp
from jax import lax
from jax.sharding import PartitionSpec as P

HD = 72
epsilon = 1e-06
negative_big = -1e30


def layer_norm(row_block, gain_vec, shift_vec):
    average = jnp.mean(row_block, -1, keepdims=True)
    center = row_block - average
    variance = jnp.mean(center * center, -1, keepdims=True)
    return center * lax.rsqrt(variance + epsilon) * gain_vec + shift_vec


def gelu_tanh(values_in):
    return jax.nn.gelu(values_in, approximate=True)


def plain_dot(left, right):
    return jnp.dot(left, right, preferred_element_type=jnp.float32)


def contract_rows(left, right):
    return lax.dot_general(
        left, right, (((0,), (0,)), ((), ())), preferred_element_type=jnp.float32
    )


def contract_cols(left, right):
    return lax.dot_general(
        left, right, (((1,), (1,)), ((), ())), preferred_element_type=jnp.float32
    )


def local(
    inputs,
    cotangent,
    lengths,
    ln1_gain,
    ln1_bias,
    q_weight,
    q_bias,
    k_weight,
    v_weight,
    v_bias,
    out_weight,
    out_bias,
    ln2_gain,
    ln2_bias,
    up_weight,
    up_bias,
    down_weight,
    down_bias,
):
    tp_count = lax.axis_size("tp")
    tp_index = lax.axis_index("tp")
    fsdp_index = lax.axis_index("fsdp")
    micro_count = inputs.shape[0]
    local_rows = inputs.shape[1]
    model_width = inputs.shape[2]
    seq_len = local_rows * tp_count
    head_width = q_weight.shape[1]
    heads_here = head_width // HD
    unit_width = up_weight.shape[1]
    scale_value = HD ** (-0.5)
    q_shift = q_bias.astype(jnp.float32)
    v_shift = v_bias.astype(jnp.float32)
    up_shift = up_bias.astype(jnp.float32)

    def fetch_weights():
        attn_full = (
            lax.all_gather(ln1_gain, "fsdp", axis=0, tiled=True),
            lax.all_gather(ln1_bias, "fsdp", axis=0, tiled=True),
            lax.all_gather(q_weight, "fsdp", axis=0, tiled=True),
            lax.all_gather(k_weight, "fsdp", axis=0, tiled=True),
            lax.all_gather(v_weight, "fsdp", axis=0, tiled=True),
            lax.all_gather(out_weight, "fsdp", axis=1, tiled=True),
            lax.all_gather(out_bias, "fsdp", axis=0, tiled=True),
        )
        mlp_full = (
            lax.all_gather(ln2_gain, "fsdp", axis=0, tiled=True),
            lax.all_gather(ln2_bias, "fsdp", axis=0, tiled=True),
            lax.all_gather(up_weight, "fsdp", axis=0, tiled=True),
            lax.all_gather(down_weight, "fsdp", axis=1, tiled=True),
            lax.all_gather(down_bias, "fsdp", axis=0, tiled=True),
        )
        return (attn_full, mlp_full)

    def masked_scores(queries, keys_all, key_valid):
        query_heads = queries.reshape(seq_len, heads_here, HD)
        key_heads = keys_all.reshape(seq_len, heads_here, HD)
        scores = (
            jnp.einsum("qhd,khd->hqk", query_heads, key_heads, preferred_element_type=jnp.float32)
            * scale_value
        )
        return jnp.where(key_valid[None, None, :], scores, negative_big)

    def forward(slot_rows, length, attn_full, mlp_full):
        gain_one, shift_one, wq_full, wk_full, wv_full, wo_full, bo_full = attn_full
        gain_two, shift_two, w_up, w_down, bd_full = mlp_full
        key_valid = jnp.arange(seq_len, dtype=jnp.int32) < length
        norm_one = layer_norm(
            slot_rows, gain_one.astype(jnp.float32), shift_one.astype(jnp.float32)
        ).astype(jnp.bfloat16)
        norm_full = lax.all_gather(norm_one, "tp", axis=0, tiled=True)
        queries = (plain_dot(norm_full, wq_full) + q_shift).astype(jnp.bfloat16)
        keys_all = plain_dot(norm_full, wk_full).astype(jnp.bfloat16)
        values_all = (plain_dot(norm_full, wv_full) + v_shift).astype(jnp.bfloat16)
        scores = masked_scores(queries, keys_all, key_valid)
        row_max = jnp.max(scores, -1, keepdims=True)
        row_total = jnp.sum(jnp.exp(scores - row_max), -1, keepdims=True)
        log_total = row_max + jnp.log(row_total)
        soft_low = jnp.exp(scores - log_total).astype(jnp.bfloat16)
        value_heads = values_all.reshape(seq_len, heads_here, HD)
        mixed_heads = jnp.einsum(
            "hqk,khd->qhd", soft_low, value_heads, preferred_element_type=jnp.float32
        )
        mixed_heads = mixed_heads.astype(jnp.bfloat16).reshape(seq_len, head_width)
        attended = lax.psum_scatter(
            plain_dot(mixed_heads, wo_full), "tp", scatter_dimension=0, tiled=True
        )
        middle = slot_rows + attended + bo_full.astype(jnp.float32)
        norm_two = layer_norm(
            middle, gain_two.astype(jnp.float32), shift_two.astype(jnp.float32)
        ).astype(jnp.bfloat16)
        norm_two_full = lax.all_gather(norm_two, "tp", axis=0, tiled=True)
        hidden = plain_dot(norm_two_full, w_up) + up_shift
        active = gelu_tanh(hidden).astype(jnp.bfloat16)
        mlp_rows = lax.psum_scatter(
            plain_dot(active, w_down), "tp", scatter_dimension=0, tiled=True
        )
        out_rows = middle + mlp_rows + bd_full.astype(jnp.float32)
        kept_state = (
            norm_full,
            queries,
            keys_all,
            values_all,
            log_total,
            mixed_heads,
            middle,
            norm_two_full,
            hidden,
            active,
        )
        return (out_rows, kept_state)

    outputs = []
    for slot_index in range(micro_count):
        attn_full, mlp_full = fetch_weights()
        out_rows, kept_state = forward(
            inputs[slot_index].astype(jnp.float32), lengths[slot_index], attn_full, mlp_full
        )
        outputs.append(out_rows.astype(jnp.bfloat16))
    grad_list = []
    totals = None
    for slot_index in range(micro_count):
        attn_full, mlp_full = fetch_weights()
        slot_rows = inputs[slot_index].astype(jnp.float32)
        kept_state = forward(slot_rows, lengths[slot_index], attn_full, mlp_full)[1]
        backward_length = lengths[slot_index]
        (
            backward_gain_one,
            backward_shift_one,
            backward_wq_full,
            backward_wk_full,
            backward_wv_full,
            backward_wo_full,
            backward_bo_full,
        ) = attn_full
        backward_gain_two, backward_shift_two, backward_w_up, backward_w_down, backward_bd_full = (
            mlp_full
        )
        (
            backward_norm_full,
            backward_queries,
            backward_keys_all,
            backward_values_all,
            backward_log_total,
            backward_mixed_heads,
            backward_middle,
            backward_norm_two_full,
            backward_hidden,
            backward_active,
        ) = kept_state
        backward_key_valid = jnp.arange(seq_len, dtype=jnp.int32) < backward_length
        row_valid = (
            jnp.arange(local_rows, dtype=jnp.int32) + tp_index * local_rows < backward_length
        ).astype(jnp.float32)
        grad_out = cotangent[slot_index].astype(jnp.float32) * row_valid[:, None]
        backward_down_sum = jnp.sum(grad_out, 0)
        grad_out_full = lax.all_gather(grad_out.astype(jnp.bfloat16), "tp", axis=0, tiled=True)
        backward_grad_w_down = contract_rows(backward_active, grad_out_full)
        grad_active = contract_cols(grad_out_full, backward_w_down)
        gelu_pull = jax.vjp(gelu_tanh, backward_hidden)[1]
        grad_hidden = gelu_pull(grad_active)[0].astype(jnp.bfloat16)
        backward_up_sum = jnp.sum(grad_hidden.astype(jnp.float32), 0)
        backward_grad_w_up = contract_rows(backward_norm_two_full, grad_hidden)
        grad_norm_two = lax.psum_scatter(
            contract_cols(grad_hidden, backward_w_up), "tp", scatter_dimension=0, tiled=True
        )
        norm_two_pull = jax.vjp(
            layer_norm,
            backward_middle,
            backward_gain_two.astype(jnp.float32),
            backward_shift_two.astype(jnp.float32),
        )[1]
        middle_part, backward_gain_two_grad, backward_shift_two_grad = norm_two_pull(grad_norm_two)
        grad_middle = grad_out + middle_part
        backward_out_sum = jnp.sum(grad_middle, 0)
        grad_middle_full = lax.all_gather(
            grad_middle.astype(jnp.bfloat16), "tp", axis=0, tiled=True
        )
        backward_grad_w_out = contract_rows(backward_mixed_heads, grad_middle_full)
        grad_mixed = (
            contract_cols(grad_middle_full, backward_wo_full)
            .astype(jnp.bfloat16)
            .reshape(seq_len, heads_here, HD)
        )
        soft_weights = jnp.exp(
            masked_scores(backward_queries, backward_keys_all, backward_key_valid)
            - backward_log_total
        )
        backward_soft_low = soft_weights.astype(jnp.bfloat16)
        backward_query_heads = backward_queries.reshape(seq_len, heads_here, HD)
        backward_key_heads = backward_keys_all.reshape(seq_len, heads_here, HD)
        backward_value_heads = backward_values_all.reshape(seq_len, heads_here, HD)
        grad_soft = jnp.einsum(
            "qhd,khd->hqk", grad_mixed, backward_value_heads, preferred_element_type=jnp.float32
        )
        row_inner = jnp.sum(soft_weights * grad_soft, -1, keepdims=True)
        grad_scores = (soft_weights * (grad_soft - row_inner)).astype(jnp.bfloat16)
        grad_queries = (
            (
                jnp.einsum(
                    "hqk,khd->qhd",
                    grad_scores,
                    backward_key_heads,
                    preferred_element_type=jnp.float32,
                )
                * scale_value
            )
            .astype(jnp.bfloat16)
            .reshape(seq_len, head_width)
        )
        grad_keys = (
            (
                jnp.einsum(
                    "hqk,qhd->khd",
                    grad_scores,
                    backward_query_heads,
                    preferred_element_type=jnp.float32,
                )
                * scale_value
            )
            .astype(jnp.bfloat16)
            .reshape(seq_len, head_width)
        )
        grad_values = (
            jnp.einsum(
                "hqk,qhd->khd", backward_soft_low, grad_mixed, preferred_element_type=jnp.float32
            )
            .astype(jnp.bfloat16)
            .reshape(seq_len, head_width)
        )
        backward_query_sum = jnp.sum(grad_queries.astype(jnp.float32), 0)
        backward_value_sum = jnp.sum(grad_values.astype(jnp.float32), 0)
        backward_grad_wq = contract_rows(backward_norm_full, grad_queries)
        backward_grad_wk = contract_rows(backward_norm_full, grad_keys)
        backward_grad_wv = contract_rows(backward_norm_full, grad_values)
        part_q = contract_cols(grad_queries, backward_wq_full)
        part_k = contract_cols(grad_keys, backward_wk_full)
        part_v = contract_cols(grad_values, backward_wv_full)
        grad_norm_one = lax.psum_scatter(
            part_q + part_k + part_v, "tp", scatter_dimension=0, tiled=True
        )
        norm_one_pull = jax.vjp(
            layer_norm,
            slot_rows,
            backward_gain_one.astype(jnp.float32),
            backward_shift_one.astype(jnp.float32),
        )[1]
        rows_part, backward_gain_one_grad, backward_shift_one_grad = norm_one_pull(grad_norm_one)
        grad_rows = grad_middle + rows_part
        slot_grads = (
            backward_gain_one_grad,
            backward_shift_one_grad,
            backward_grad_wq,
            backward_query_sum,
            backward_grad_wk,
            backward_grad_wv,
            backward_value_sum,
            backward_grad_w_out,
            backward_out_sum,
            backward_gain_two_grad,
            backward_shift_two_grad,
            backward_grad_w_up,
            backward_up_sum,
            backward_grad_w_down,
            backward_down_sum,
        )
        grad_rows, slot_grads = (grad_rows, slot_grads)
        grad_list.append(grad_rows)
        if totals is None:
            totals = slot_grads
        else:
            totals = jax.tree.map(jnp.add, totals, slot_grads)
    (
        gain_one_grad,
        shift_one_grad,
        grad_wq,
        query_sum,
        grad_wk,
        grad_wv,
        value_sum,
        grad_w_out,
        out_sum,
        gain_two_grad,
        shift_two_grad,
        grad_w_up,
        up_sum,
        grad_w_down,
        down_sum,
    ) = totals
    summed_weights = (
        lax.psum_scatter(grad_wq, "fsdp", scatter_dimension=0, tiled=True),
        lax.psum_scatter(grad_wk, "fsdp", scatter_dimension=0, tiled=True),
        lax.psum_scatter(grad_wv, "fsdp", scatter_dimension=0, tiled=True),
        lax.psum_scatter(grad_w_out, "fsdp", scatter_dimension=1, tiled=True),
        lax.psum_scatter(grad_w_up, "fsdp", scatter_dimension=0, tiled=True),
        lax.psum_scatter(grad_w_down, "fsdp", scatter_dimension=1, tiled=True),
    )
    width_stack = jnp.stack(
        [gain_one_grad, shift_one_grad, out_sum, gain_two_grad, shift_two_grad, down_sum], 0
    )
    head_stack = jnp.zeros((2, head_width * tp_count), jnp.float32)
    head_stack = lax.dynamic_update_slice_in_dim(
        head_stack, jnp.stack([query_sum, value_sum], 0), tp_index * head_width, 1
    )
    unit_line = jnp.zeros((unit_width * tp_count,), jnp.float32)
    unit_line = lax.dynamic_update_slice_in_dim(unit_line, up_sum, tp_index * unit_width, 0)
    summed_small = lax.psum((width_stack, head_stack, unit_line), ("fsdp", "tp"))
    shard_size = model_width // lax.axis_size("fsdp")
    width_pieces = lax.dynamic_slice_in_dim(summed_small[0], fsdp_index * shard_size, shard_size, 1)
    head_pieces = lax.dynamic_slice_in_dim(summed_small[1], tp_index * head_width, head_width, 1)
    unit_piece = lax.dynamic_slice_in_dim(summed_small[2], tp_index * unit_width, unit_width, 0)
    return (
        jnp.stack(outputs, 0),
        jnp.stack(grad_list, 0),
        width_pieces[0],
        width_pieces[1],
        summed_weights[0],
        head_pieces[0],
        summed_weights[1],
        summed_weights[2],
        head_pieces[1],
        summed_weights[3],
        width_pieces[2],
        width_pieces[3],
        width_pieces[4],
        summed_weights[4],
        unit_piece,
        summed_weights[5],
        width_pieces[5],
    )


def solution(mesh):
    in_specs = (
        P("fsdp", "tp", None),
        P("fsdp", "tp", None),
        P("fsdp"),
        P("fsdp"),
        P("fsdp"),
        P("fsdp", "tp"),
        P("tp"),
        P("fsdp", "tp"),
        P("fsdp", "tp"),
        P("tp"),
        P("tp", "fsdp"),
        P("fsdp"),
        P("fsdp"),
        P("fsdp"),
        P("fsdp", "tp"),
        P("tp"),
        P("tp", "fsdp"),
        P("fsdp"),
    )
    out_specs = (
        P("fsdp", "tp", None),
        P("fsdp", "tp", None),
        P("fsdp"),
        P("fsdp"),
        P("fsdp", "tp"),
        P("tp"),
        P("fsdp", "tp"),
        P("fsdp", "tp"),
        P("tp"),
        P("tp", "fsdp"),
        P("fsdp"),
        P("fsdp"),
        P("fsdp"),
        P("fsdp", "tp"),
        P("tp"),
        P("tp", "fsdp"),
        P("fsdp"),
    )
    return jax.shard_map(local, mesh=mesh, in_specs=in_specs, out_specs=out_specs, check_vma=False)
```

profile of v0, /device:TPU:0, one launch (start us, length us, event | category | flops | bytes accessed | tf_op | source)
XLA Modules:
  0.0 1294.0 jit_solution(5558494795576318744)
XLA Ops:
  14.4 38.8 %all-reduce.15 = (bf16[1152]{0:T(1024)(128)(2,1)S(1)}, bf16[1152]{0:T(1024)(128)(2,1)S(1)}, bf16[1152]{0:T(1024)(128)(2,1)S(1)}, bf16[1152]{0:T(1024)(128)(2,1)S...) all-reduce(bf16[1152]{0:T(1024)(128)(2,1)S(1)} %dynamic-update-slic, ...), channel_id=1, replica_groups=mesh['fsdp'=8,'tp'=4] {'fsdp'}, use_global_device_ids=true, to_apply=%add.1 | all-reduce | flops 6912 | bytes 27648
  60.0 32.5 %all_gather.44 = bf16[1152,288]{1,0:T(8,128)(2,1)S(1)} all-gather(bf16[144,288]{1,0:T(8,128)(2,1)S(1)} %copy-done.54), channel_id=1, replica_groups=mesh['fsdp'=8,'tp'=4] {'fsdp'}, dimensions={0}, use_global_device_ids=true | all-gather | bytes 746496 | tf_op jit(solution)/shard_map/all_gather | solution.py:77
  92.5 32.2 %all_gather.45 = bf16[1152,288]{1,0:T(8,128)(2,1)S(1)} all-gather(bf16[144,288]{1,0:T(8,128)(2,1)S(1)} %copy-done.55), channel_id=1, replica_groups=mesh['fsdp'=8,'tp'=4] {'fsdp'}, dimensions={0}, use_global_device_ids=true | all-gather | bytes 746496 | tf_op jit(solution)/shard_map/all_gather | solution.py:78
  126.1 34.5 %all_gather.43 = bf16[1152,288]{1,0:T(8,128)(2,1)} all-gather(bf16[144,288]{1,0:T(8,128)(2,1)S(1)} %copy-done.56), channel_id=1, replica_groups=mesh['fsdp'=8,'tp'=4] {'fsdp'}, dimensions={0}, use_global_device_ids=true | all-gather | bytes 746496 | tf_op jit(solution)/shard_map/all_gather | solution.py:79
  160.6 32.0 %all_gather.46 = bf16[288,1152]{0,1:T(8,128)(2,1)S(1)} all-gather(bf16[288,144]{0,1:T(8,128)(2,1)S(1)} %copy-done.57), channel_id=1, replica_groups=mesh['fsdp'=8,'tp'=4] {'fsdp'}, dimensions={1}, use_global_device_ids=true | all-gather | bytes 746496 | tf_op jit(solution)/shard_map/all_gather | solution.py:80
  231.9 15.0 %reduce-scatter.47.cloned.1.call-done = f32[184,1152]{1,0:T(8,128)} async-done(((f32[736,1152]{1,0:T(8,128)}), f32[184,1152]{1,0:T(8,128)}) %reduce-scatter.47.cloned.1.call-update) | async-done | bytes 847888
  247.0 42.0 %reduce-scatter.43.cloned.1.call-done = f32[184,1152]{1,0:T(8,128)} async-done(((f32[736,1152]{1,0:T(8,128)}), f32[184,1152]{1,0:T(8,128)}) %reduce-scatter.43.cloned.1.call-update) | async-done | bytes 847888
  294.4 17.0 %all-gather.23.cloned.1.call-done = bf16[736,1152]{1,0:T(8,128)(2,1)} async-done(((bf16[184,1152]{1,0:T(8,128)(2,1)}), bf16[736,1152]{1,0:T(8,128)(2,1)}) %all-gather.23.cloned.1.call-update) | async-done | bytes 1695760 | tf_op jit(solution)/shard_map/all_gather | solution.py:194
  311.4 57.1 %all-gather.17.cloned.1.call-done = bf16[1076,1152]{0,1:T(8,128)(2,1)} async-done(((bf16[1076,144]{0,1:T(8,128)(2,1)}), bf16[1076,1152]{0,1:T(8,128)(2,1)}) %all-gather.17.cloned.1.call-update) | async-done | bytes 2479120 | tf_op jit(solution)/shard_map/all_gather | solution.py:87
  368.5 6.4 fusion.87
  374.9 49.4 %all-gather.15.cloned.1.call-done = bf16[1152,1076]{1,0:T(8,128)(2,1)} async-done(((bf16[144,1076]{1,0:T(8,128)(2,1)}), bf16[1152,1076]{1,0:T(8,128)(2,1)}) %all-gather.15.cloned.1.call-update) | async-done | bytes 2479120 | tf_op jit(solution)/shard_map/all_gather | solution.py:86
  424.3 20.5 %all-gather.13.cloned.1.call-done = bf16[736,1152]{1,0:T(8,128)(2,1)} async-done(((bf16[184,1152]{1,0:T(8,128)(2,1)}), bf16[736,1152]{1,0:T(8,128)(2,1)}) %all-gather.13.cloned.1.call-update) | async-done | bytes 1695760 | tf_op jit(solution)/shard_map/all_gather | solution.py:129
  444.8 10.3 convert_reduce_fusion.1
  466.7 6.4 fusion.90
  473.1 15.4 %all-gather.21.cloned.1.call-done = bf16[736,1152]{1,0:T(8,128)(2,1)} async-done(((bf16[184,1152]{1,0:T(8,128)(2,1)}), bf16[736,1152]{1,0:T(8,128)(2,1)}) %all-gather.21.cloned.1.call-update) | async-done | bytes 1695760 | tf_op jit(solution)/shard_map/all_gather | solution.py:129
  488.5 10.2 convert_reduce_fusion
  504.6 7.8 fusion.73
  512.5 7.6 fusion.74
  520.2 10.4 reduce-scatter.51.cloned.1.call-done
  530.6 42.1 %reduce-scatter.55.cloned.1.call-done = f32[184,1152]{1,0:T(8,128)} async-done(((f32[736,1152]{1,0:T(8,128)}), f32[184,1152]{1,0:T(8,128)}) %reduce-scatter.55.cloned.1.call-update) | async-done | bytes 847888
  574.8 39.9 %reduce-scatter.45.cloned.1.call-done = f32[184,1152]{1,0:T(8,128)} async-done(((f32[736,1152]{1,0:T(8,128)}), f32[184,1152]{1,0:T(8,128)}) %reduce-scatter.45.cloned.1.call-update) | async-done | bytes 847888
  614.7 42.1 %reduce-scatter.49.cloned.1.call-done = f32[184,1152]{1,0:T(8,128)} async-done(((f32[736,1152]{1,0:T(8,128)}), f32[184,1152]{1,0:T(8,128)}) %reduce-scatter.49.cloned.1.call-update) | async-done | bytes 847888
  665.4 19.5 %all-gather.29.cloned.1.call-done = bf16[736,1152]{1,0:T(8,128)(2,1)} async-done(((bf16[184,1152]{1,0:T(8,128)(2,1)}), bf16[736,1152]{1,0:T(8,128)(2,1)}) %all-gather.29.cloned.1.call-update) | async-done | bytes 1695760 | tf_op jit(solution)/shard_map/all_gather | solution.py:213
  713.2 6.6 multiply_reduce_fusion.1
  782.2 9.3 reduce-scatter.53.cloned.1.call-done
  796.5 43.7 %all-reduce.14 = (f32[6,1152]{1,0:T(8,128)}, f32[2,1152]{1,0:T(2,128)S(1)}, f32[4304]{0:T(1024)S(1)}) all-reduce(f32[6,1152]{1,0:T(8,128)S(1)} %stack.38, f32[2,1152]{1,0:T(2,128)S(1)} %dynamic_update_slice.6, f32[4304]{0:T(1024)S(1)} %add_dynamic-update-slice_fusion), channel_id=1, replica_groups=mesh['fsdp'=8,'tp'=4] {'fsdp','tp'}, use_global_device_ids=true, to_apply=%region_42.43 | all-reduce | flops 13520 | bytes 108160 | tf_op jit(solution)/shard_map/psum | solution.py:344
  848.7 52.2 %reduce-scatter.39.cloned.1.call-done = f32[144,1076]{1,0:T(8,128)} async-done(((f32[1152,1076]{1,0:T(8,128)}), f32[144,1076]{1,0:T(8,128)}) %reduce-scatter.39.cloned.1.call-update) | async-done | bytes 619792 | tf_op jit(solution)/shard_map/reduce_scatter | solution.py:332
  901.0 108.4 %reduce-scatter.41.cloned.1.call-done = f32[1076,144]{0,1:T(8,128)} async-done(((f32[1076,1152]{0,1:T(8,128)}), f32[1076,144]{0,1:T(8,128)}) %reduce-scatter.41.cloned.1.call-update) | async-done | bytes 619792 | tf_op jit(solution)/shard_map/reduce_scatter | solution.py:333
  1009.4 69.9 %reduce-scatter.37.cloned.1.call-done = f32[288,144]{0,1:T(8,128)} async-done(((f32[288,1152]{0,1:T(8,128)}), f32[288,144]{0,1:T(8,128)}) %reduce-scatter.37.cloned.1.call-update) | async-done | bytes 165904 | tf_op jit(solution)/shard_map/reduce_scatter | solution.py:331
  1079.3 69.5 %reduce-scatter.35.cloned.1.call-done = f32[144,288]{1,0:T(8,128)} async-done(((f32[1152,288]{1,0:T(8,128)}), f32[144,288]{1,0:T(8,128)}) %reduce-scatter.35.cloned.1.call-update) | async-done | bytes 165904 | tf_op jit(solution)/shard_map/reduce_scatter | solution.py:330
  1148.7 69.0 %reduce-scatter.33.cloned.1.call-done = f32[144,288]{1,0:T(8,128)} async-done(((f32[1152,288]{1,0:T(8,128)}), f32[144,288]{1,0:T(8,128)}) %reduce-scatter.33.cloned.1.call-update) | async-done | bytes 165904 | tf_op jit(solution)/shard_map/reduce_scatter | solution.py:329
  1217.7 69.0 %reduce-scatter.31.cloned.1.call-done = f32[144,288]{1,0:T(8,128)} async-done(((f32[1152,288]{1,0:T(8,128)}), f32[144,288]{1,0:T(8,128)}) %reduce-scatter.31.cloned.1.call-update) | async-done | bytes 165904 | tf_op jit(solution)/shard_map/reduce_scatter | solution.py:328
  (417 shorter events, 190.1 us)
Async XLA Ops:
  7.2 85.3 %copy-start.91 = (bf16[288]{0:T(512)(128)(2,1)S(1)}, bf16[288]{0:T(512)(128)(2,1)}, u32[]{:S(2)}) copy-start(bf16[288]{0:T(512)(128)(2,1)} %param.24) | copy-start | bytes 1732
  7.2 117.5 %copy-start.90 = (s32[2]{0:T(128)S(1)}, s32[2]{0:T(128)}, u32[]{:S(2)}) copy-start(s32[2]{0:T(128)} %param.20) | copy-start | bytes 28
  7.2 118.8 %copy-start.56 = (bf16[144,288]{1,0:T(8,128)(2,1)S(1)}, bf16[144,288]{1,0:T(8,128)(2,1)}, u32[]{:S(2)}) copy-start(bf16[144,288]{1,0:T(8,128)(2,1)} %param.26) | copy-start | bytes 248836
  7.2 185.3 %all-gather.19.cloned.1.call-start = ((), (), s32[]{:S(2)}) async-start(), calls=%async_computation.18 | async-start | bytes 2119680 | tf_op jit(solution)/shard_map/all_gather | solution.py:108
  54.6 106.0 %copy-start.92 = (bf16[288]{0:T(512)(128)(2,1)S(1)}, bf16[288]{0:T(512)(128)(2,1)}, u32[]{:S(2)}) copy-start(bf16[288]{0:T(512)(128)(2,1)} %param.27) | copy-start | bytes 1732
  54.6 106.0 %copy-start.57 = (bf16[288,144]{0,1:T(8,128)(2,1)S(1)}, bf16[288,144]{0,1:T(8,128)(2,1)}, u32[]{:S(2)}) copy-start(bf16[288,144]{0,1:T(8,128)(2,1)} %param.28) | copy-start | bytes 248836
  59.2 151.7 %all-gather.11.cloned.1.call-start = ((), (), s32[]{:S(2)}) async-start(), calls=%async_computation.14 | async-start | bytes 2119680 | tf_op jit(solution)/shard_map/all_gather | solution.py:108
  60.0 187.0 %reduce-scatter.47.cloned.1.call-start = ((), (), s32[]{:S(2)}) async-start(), calls=%async_computation.32 | async-start | bytes 4239360
  124.7 86.1 %copy-start.11 = (bf16[1152,288]{1,0:T(8,128)(2,1)}, bf16[1152,288]{1,0:T(8,128)(2,1)S(1)}, u32[]{:S(2)}) copy-start(bf16[1152,288]{1,0:T(8,128)(2,1)S(1)} %all_gather.45) | copy-start | bytes 1990660
  209.9 79.2 %reduce-scatter.43.cloned.1.call-start = ((), (), s32[]{:S(2)}) async-start(), calls=%async_computation.30 | async-start | bytes 4239360
  227.8 83.6 %all-gather.23.cloned.1.call-start = ((), (), s32[]{:S(2)}) async-start(), calls=%async_computation.20 | async-start | bytes 2119680 | tf_op jit(solution)/shard_map/all_gather | solution.py:194
  230.5 138.0 %all-gather.17.cloned.1.call-start = ((), (), s32[]{:S(2)}) async-start(), calls=%async_computation.17 | async-start | bytes 2985984 | tf_op jit(solution)/shard_map/all_gather | solution.py:87
  231.1 193.2 %all-gather.15.cloned.1.call-start = ((), (), s32[]{:S(2)}) async-start(), calls=%async_computation.16 | async-start | bytes 2985984 | tf_op jit(solution)/shard_map/all_gather | solution.py:86
  231.8 213.0 %all-gather.13.cloned.1.call-start = ((), (), s32[]{:S(2)}) async-start(), calls=%async_computation.15 | async-start | bytes 2119680 | tf_op jit(solution)/shard_map/all_gather | solution.py:129
  292.6 174.2 %all-gather.27.cloned.1.call-start = ((), (), s32[]{:S(2)}) async-start(), calls=%async_computation.22 | async-start | bytes 2119680 | tf_op jit(solution)/shard_map/all_gather | solution.py:194
  293.3 195.2 %all-gather.21.cloned.1.call-start = ((), (), s32[]{:S(2)}) async-start(), calls=%async_computation.19 | async-start | bytes 2119680 | tf_op jit(solution)/shard_map/all_gather | solution.py:129
  293.9 236.7 %reduce-scatter.51.cloned.1.call-start = ((), (), s32[]{:S(2)}) async-start(), calls=%async_computation.34 | async-start | bytes 4239360
  460.8 111.9 %reduce-scatter.55.cloned.1.call-start = ((), (), s32[]{:S(2)}) async-start(), calls=%async_computation.36 | async-start | bytes 4239360
  504.3 110.3 %reduce-scatter.45.cloned.1.call-start = ((), (), s32[]{:S(2)}) async-start(), calls=%async_computation.31 | async-start | bytes 4239360
  512.4 144.3 %reduce-scatter.49.cloned.1.call-start = ((), (), s32[]{:S(2)}) async-start(), calls=%async_computation.33 | async-start | bytes 4239360
  520.1 164.7 %all-gather.29.cloned.1.call-start = ((), (), s32[]{:S(2)}) async-start(), calls=%async_computation.23 | async-start | bytes 2119680 | tf_op jit(solution)/shard_map/all_gather | solution.py:213
  574.7 86.5 %copy-start.72 = (f32[184]{0:T(256)S(1)}, f32[184]{0:T(256)}, u32[]{:S(2)}) copy-start(f32[184]{0:T(256)} %copy-done.71) | copy-start | bytes 2212
  574.7 86.5 %copy-start.75 = (f32[184]{0:T(256)S(1)}, f32[184]{0:T(256)}, u32[]{:S(2)}) copy-start(f32[184]{0:T(256)} %copy-done.74) | copy-start | bytes 2212
  664.4 45.6 %all-gather.25.cloned.1.call-start = ((), (), s32[]{:S(2)}) async-start(), calls=%async_computation.21 | async-start | bytes 2119680 | tf_op jit(solution)/shard_map/all_gather | solution.py:213
  665.0 117.2 %reduce-scatter.57.cloned.1.call-start = ((), (), s32[]{:S(2)}) async-start(), calls=%async_computation.37 | async-start | bytes 4239360
  709.8 81.7 %reduce-scatter.53.cloned.1.call-start = ((), (), s32[]{:S(2)}) async-start(), calls=%async_computation.35 | async-start | bytes 4239360
  734.7 166.2 %reduce-scatter.39.cloned.1.call-start = ((), (), s32[]{:S(2)}) async-start(), calls=%async_computation.28 | async-start | bytes 5971968 | tf_op jit(solution)/shard_map/reduce_scatter | solution.py:332
  745.5 263.9 %reduce-scatter.41.cloned.1.call-start = ((), (), s32[]{:S(2)}) async-start(), calls=%async_computation.29 | async-start | bytes 5971968 | tf_op jit(solution)/shard_map/reduce_scatter | solution.py:333
  756.8 322.4 %reduce-scatter.37.cloned.1.call-start = ((), (), s32[]{:S(2)}) async-start(), calls=%async_computation.27 | async-start | bytes 1990656 | tf_op jit(solution)/shard_map/reduce_scatter | solution.py:331
  763.1 385.7 %reduce-scatter.35.cloned.1.call-start = ((), (), s32[]{:S(2)}) async-start(), calls=%async_computation.26 | async-start | bytes 1990656 | tf_op jit(solution)/shard_map/reduce_scatter | solution.py:330
  768.3 449.4 %reduce-scatter.33.cloned.1.call-start = ((), (), s32[]{:S(2)}) async-start(), calls=%async_computation.25 | async-start | bytes 1990656 | tf_op jit(solution)/shard_map/reduce_scatter | solution.py:329
  773.5 513.2 %reduce-scatter.31.cloned.1.call-start = ((), (), s32[]{:S(2)}) async-start(), calls=%async_computation.24 | async-start | bytes 1990656 | tf_op jit(solution)/shard_map/reduce_scatter | solution.py:328
  (106 other events, 1012.5 us)
Sparse Core Ops, SparseCore 0:
  59.3 17.5 all-gather.18
  79.0 20.3 all-gather.10
  210.0 36.9 reduce-scatter.46
  249.5 39.4 reduce-scatter.42
  291.0 20.3 all-gather.22
  313.4 55.0 all-gather.16
  370.6 53.5 all-gather.14
  425.8 18.9 all-gather.12
  446.4 20.3 all-gather.26
  468.1 20.3 all-gather.20
  491.1 39.4 reduce-scatter.50
  533.1 39.4 reduce-scatter.54
  575.2 39.4 reduce-scatter.44
  617.2 39.4 reduce-scatter.48
  664.5 20.3 all-gather.28
  686.3 20.3 all-gather.24
  709.9 39.4 reduce-scatter.56
  752.0 39.4 reduce-scatter.52
  795.6 105.2 reduce-scatter.38
  905.4 103.9 reduce-scatter.40
  1013.4 65.7 reduce-scatter.36
  1083.7 64.9 reduce-scatter.34
  1152.8 64.8 reduce-scatter.32
  1222.0 64.6 reduce-scatter.30
where the time goes:
time: 1300 us; the launch traced here: 1290 us
  waiting for transfers between devices  827 us (64%)
  blocking collectives  214 us (16%)
  matrix products  156 us (12%)
  other arithmetic  50 us (4%)
  local copies, waits for them, and re-layouts  26.7 us (2%)
  between operations  17.3 us (1%)
    unnamed x32, waiting for transfers between devices  205 us
    reduce_scatter x1, waiting for transfers between devices, local(): lax.psum_scatter(grad_w_down, 'fsdp', scatter_dimension=1, tiled=True)  108 us
    reduce_scatter x1, waiting for transfers between devices, local(): lax.psum_scatter(grad_w_out, 'fsdp', scatter_dimension=1, tiled=True)  69.9 us
    reduce_scatter x1, waiting for transfers between devices, local(): lax.psum_scatter(grad_wv, 'fsdp', scatter_dimension=0, tiled=True)  69.5 us
    reduce_scatter x1, waiting for transfers between devices, local(): lax.psum_scatter(grad_wq, 'fsdp', scatter_dimension=0, tiled=True)  69 us
    reduce_scatter x1, waiting for transfers between devices, local(): lax.psum_scatter(grad_wk, 'fsdp', scatter_dimension=0, tiled=True)  69 us
    all_gather x1, waiting for transfers between devices, fetch_weights(): lax.all_gather(down_weight, 'fsdp', axis=1, tiled=True)  57.1 us
    reduce_scatter x1, waiting for transfers between devices, local(): lax.psum_scatter(grad_w_up, 'fsdp', scatter_dimension=0, tiled=True)  52.2 us
  transfers between devices with their start and end apart: 24, of which 20 were waited for; matrix products, arithmetic and copies ran while one was open for 15% of the time, Pallas kernels for 0%

commit v1 on v0

--- a/solution.py
+++ b/solution.py
@@ -341,7 +341,8 @@
     )
     unit_line = jnp.zeros((unit_width * tp_count,), jnp.float32)
     unit_line = lax.dynamic_update_slice_in_dim(unit_line, up_sum, tp_index * unit_width, 0)
-    summed_small = lax.psum((width_stack, head_stack, unit_line), ("fsdp", "tp"))
+    inner = lax.psum((width_stack, head_stack, unit_line), "tp")
+    summed_small = lax.psum(inner, "fsdp")
     shard_size = model_width // lax.axis_size("fsdp")
     width_pieces = lax.dynamic_slice_in_dim(summed_small[0], fsdp_index * shard_size, shard_size, 1)
     head_pieces = lax.dynamic_slice_in_dim(summed_small[1], tp_index * head_width, head_width, 1)

time: 1300 us -> 1300 us (level)
    psum x1 -> x2, blocking collectives: 43.7 us -> 53.3 us  [the longest x1 42.3 us: local(): summed_small = lax.psum(inner, 'fsdp')]
where the time goes in v1:
time: 1300 us
  waiting for transfers between devices  820 us (63%)
  blocking collectives  223 us (17%)
  matrix products  156 us (12%)
  other arithmetic  50.1 us (4%)
  local copies, waits for them, and re-layouts  25.8 us (2%)
  between operations  17.3 us (1%)
    unnamed x32, waiting for transfers between devices  205 us
    reduce_scatter x1, waiting for transfers between devices, local(): lax.psum_scatter(grad_w_down, 'fsdp', scatter_dimension=1, tiled=True)  108 us
    reduce_scatter x1, waiting for transfers between devices, local(): lax.psum_scatter(grad_w_out, 'fsdp', scatter_dimension=1, tiled=True)  70 us
    reduce_scatter x1, waiting for transfers between devices, local(): lax.psum_scatter(grad_wv, 'fsdp', scatter_dimension=0, tiled=True)  69.5 us
    reduce_scatter x1, waiting for transfers between devices, local(): lax.psum_scatter(grad_wq, 'fsdp', scatter_dimension=0, tiled=True)  69.4 us
    reduce_scatter x1, waiting for transfers between devices, local(): lax.psum_scatter(grad_wk, 'fsdp', scatter_dimension=0, tiled=True)  69.3 us
    all_gather x1, waiting for transfers between devices, fetch_weights(): lax.all_gather(down_weight, 'fsdp', axis=1, tiled=True)  57.1 us
    dot_general x12, matrix products, plain_dot(): return jnp.dot(left, right, preferred_element_type=jnp.float32)  49.9 us
  transfers between devices with their start and end apart: 24, of which 20 were waited for; matrix products, arithmetic and copies ran while one was open for 15% of the time, Pallas kernels for 0%

profile of v1, /device:TPU:0, one launch (start us, length us, event | category | flops | bytes accessed | tf_op | source)
XLA Modules:
  0.0 1295.7 jit_solution(14003539334269352539)
XLA Ops:
  14.4 38.8 %all-reduce.16 = (bf16[1152]{0:T(1024)(128)(2,1)S(1)}, bf16[1152]{0:T(1024)(128)(2,1)S(1)}, bf16[1152]{0:T(1024)(128)(2,1)S(1)}, bf16[1152]{0:T(1024)(128)(2,1)S...) all-reduce(bf16[1152]{0:T(1024)(128)(2,1)S(1)} %dynamic-update-slic, ...), channel_id=1, replica_groups=mesh['fsdp'=8,'tp'=4] {'fsdp'}, use_global_device_ids=true, to_apply=%add.1 | all-reduce | flops 6912 | bytes 27648
  60.0 32.5 %all_gather.44 = bf16[1152,288]{1,0:T(8,128)(2,1)S(1)} all-gather(bf16[144,288]{1,0:T(8,128)(2,1)S(1)} %copy-done.54), channel_id=1, replica_groups=mesh['fsdp'=8,'tp'=4] {'fsdp'}, dimensions={0}, use_global_device_ids=true | all-gather | bytes 746496 | tf_op jit(solution)/shard_map/all_gather | solution.py:77
  92.5 32.2 %all_gather.45 = bf16[1152,288]{1,0:T(8,128)(2,1)S(1)} all-gather(bf16[144,288]{1,0:T(8,128)(2,1)S(1)} %copy-done.55), channel_id=1, replica_groups=mesh['fsdp'=8,'tp'=4] {'fsdp'}, dimensions={0}, use_global_device_ids=true | all-gather | bytes 746496 | tf_op jit(solution)/shard_map/all_gather | solution.py:78
  126.1 34.5 %all_gather.43 = bf16[1152,288]{1,0:T(8,128)(2,1)} all-gather(bf16[144,288]{1,0:T(8,128)(2,1)S(1)} %copy-done.56), channel_id=1, replica_groups=mesh['fsdp'=8,'tp'=4] {'fsdp'}, dimensions={0}, use_global_device_ids=true | all-gather | bytes 746496 | tf_op jit(solution)/shard_map/all_gather | solution.py:79
  160.6 32.0 %all_gather.46 = bf16[288,1152]{0,1:T(8,128)(2,1)S(1)} all-gather(bf16[288,144]{0,1:T(8,128)(2,1)S(1)} %copy-done.57), channel_id=1, replica_groups=mesh['fsdp'=8,'tp'=4] {'fsdp'}, dimensions={1}, use_global_device_ids=true | all-gather | bytes 746496 | tf_op jit(solution)/shard_map/all_gather | solution.py:80
  231.9 15.1 %reduce-scatter.47.cloned.1.call-done = f32[184,1152]{1,0:T(8,128)} async-done(((f32[736,1152]{1,0:T(8,128)}), f32[184,1152]{1,0:T(8,128)}) %reduce-scatter.47.cloned.1.call-update) | async-done | bytes 847888
  247.0 42.0 %reduce-scatter.43.cloned.1.call-done = f32[184,1152]{1,0:T(8,128)} async-done(((f32[736,1152]{1,0:T(8,128)}), f32[184,1152]{1,0:T(8,128)}) %reduce-scatter.43.cloned.1.call-update) | async-done | bytes 847888
  294.5 16.9 %all-gather.23.cloned.1.call-done = bf16[736,1152]{1,0:T(8,128)(2,1)} async-done(((bf16[184,1152]{1,0:T(8,128)(2,1)}), bf16[736,1152]{1,0:T(8,128)(2,1)}) %all-gather.23.cloned.1.call-update) | async-done | bytes 1695760 | tf_op jit(solution)/shard_map/all_gather | solution.py:194
  311.5 57.1 %all-gather.17.cloned.1.call-done = bf16[1076,1152]{0,1:T(8,128)(2,1)} async-done(((bf16[1076,144]{0,1:T(8,128)(2,1)}), bf16[1076,1152]{0,1:T(8,128)(2,1)}) %all-gather.17.cloned.1.call-update) | async-done | bytes 2479120 | tf_op jit(solution)/shard_map/all_gather | solution.py:87
  368.5 6.4 fusion.87
  375.0 49.4 %all-gather.15.cloned.1.call-done = bf16[1152,1076]{1,0:T(8,128)(2,1)} async-done(((bf16[144,1076]{1,0:T(8,128)(2,1)}), bf16[1152,1076]{1,0:T(8,128)(2,1)}) %all-gather.15.cloned.1.call-update) | async-done | bytes 2479120 | tf_op jit(solution)/shard_map/all_gather | solution.py:86
  424.3 20.5 %all-gather.13.cloned.1.call-done = bf16[736,1152]{1,0:T(8,128)(2,1)} async-done(((bf16[184,1152]{1,0:T(8,128)(2,1)}), bf16[736,1152]{1,0:T(8,128)(2,1)}) %all-gather.13.cloned.1.call-update) | async-done | bytes 1695760 | tf_op jit(solution)/shard_map/all_gather | solution.py:129
  444.9 10.3 convert_reduce_fusion.1
  473.2 15.4 %all-gather.21.cloned.1.call-done = bf16[736,1152]{1,0:T(8,128)(2,1)} async-done(((bf16[184,1152]{1,0:T(8,128)(2,1)}), bf16[736,1152]{1,0:T(8,128)(2,1)}) %all-gather.21.cloned.1.call-update) | async-done | bytes 1695760 | tf_op jit(solution)/shard_map/all_gather | solution.py:129
  488.6 10.2 convert_reduce_fusion
  504.7 7.8 fusion.73
  512.5 7.6 fusion.74
  520.3 10.4 reduce-scatter.51.cloned.1.call-done
  530.6 42.1 %reduce-scatter.55.cloned.1.call-done = f32[184,1152]{1,0:T(8,128)} async-done(((f32[736,1152]{1,0:T(8,128)}), f32[184,1152]{1,0:T(8,128)}) %reduce-scatter.55.cloned.1.call-update) | async-done | bytes 847888
  574.8 39.9 %reduce-scatter.45.cloned.1.call-done = f32[184,1152]{1,0:T(8,128)} async-done(((f32[736,1152]{1,0:T(8,128)}), f32[184,1152]{1,0:T(8,128)}) %reduce-scatter.45.cloned.1.call-update) | async-done | bytes 847888
  614.8 42.1 %reduce-scatter.49.cloned.1.call-done = f32[184,1152]{1,0:T(8,128)} async-done(((f32[736,1152]{1,0:T(8,128)}), f32[184,1152]{1,0:T(8,128)}) %reduce-scatter.49.cloned.1.call-update) | async-done | bytes 847888
  665.4 19.5 %all-gather.29.cloned.1.call-done = bf16[736,1152]{1,0:T(8,128)(2,1)} async-done(((bf16[184,1152]{1,0:T(8,128)(2,1)}), bf16[736,1152]{1,0:T(8,128)(2,1)}) %all-gather.29.cloned.1.call-update) | async-done | bytes 1695760 | tf_op jit(solution)/shard_map/all_gather | solution.py:213
  713.3 6.6 multiply_reduce_fusion.1
  782.2 9.3 reduce-scatter.53.cloned.1.call-done
  796.6 11.0 all-reduce.15
  807.6 42.3 %all-reduce.14 = (f32[6,1152]{1,0:T(8,128)S(1)}, f32[2,1152]{1,0:T(2,128)S(1)}, f32[4304]{0:T(1024)S(1)}) all-reduce(f32[6,1152]{1,0:T(8,128)S(1)} %get-tuple-element.48, f32[2,1152]{1,0:T(2,128)S(1)} %get-tuple-element.49, f32[4304]{0:T(1024)S(1)} %get-tuple-element.50), channel_id=1, replica_groups=mesh['fsdp'=8,'tp'=4] {'fsdp'}, use_global_device_ids=true, to_apply=%region_43.44 | all-reduce | flops 13520 | bytes 108160 | tf_op jit(solution)/shard_map/psum | solution.py:345
  857.5 44.4 %reduce-scatter.39.cloned.1.call-done = f32[144,1076]{1,0:T(8,128)} async-done(((f32[1152,1076]{1,0:T(8,128)}), f32[144,1076]{1,0:T(8,128)}) %reduce-scatter.39.cloned.1.call-update) | async-done | bytes 619792 | tf_op jit(solution)/shard_map/reduce_scatter | solution.py:332
  901.9 108.4 %reduce-scatter.41.cloned.1.call-done = f32[1076,144]{0,1:T(8,128)} async-done(((f32[1076,1152]{0,1:T(8,128)}), f32[1076,144]{0,1:T(8,128)}) %reduce-scatter.41.cloned.1.call-update) | async-done | bytes 619792 | tf_op jit(solution)/shard_map/reduce_scatter | solution.py:333
  1010.4 70.0 %reduce-scatter.37.cloned.1.call-done = f32[288,144]{0,1:T(8,128)} async-done(((f32[288,1152]{0,1:T(8,128)}), f32[288,144]{0,1:T(8,128)}) %reduce-scatter.37.cloned.1.call-update) | async-done | bytes 165904 | tf_op jit(solution)/shard_map/reduce_scatter | solution.py:331
  1080.3 69.5 %reduce-scatter.35.cloned.1.call-done = f32[144,288]{1,0:T(8,128)} async-done(((f32[1152,288]{1,0:T(8,128)}), f32[144,288]{1,0:T(8,128)}) %reduce-scatter.35.cloned.1.call-update) | async-done | bytes 165904 | tf_op jit(solution)/shard_map/reduce_scatter | solution.py:330
  1149.8 69.3 %reduce-scatter.33.cloned.1.call-done = f32[144,288]{1,0:T(8,128)} async-done(((f32[1152,288]{1,0:T(8,128)}), f32[144,288]{1,0:T(8,128)}) %reduce-scatter.33.cloned.1.call-update) | async-done | bytes 165904 | tf_op jit(solution)/shard_map/reduce_scatter | solution.py:329
  1219.1 69.4 %reduce-scatter.31.cloned.1.call-done = f32[144,288]{1,0:T(8,128)} async-done(((f32[1152,288]{1,0:T(8,128)}), f32[144,288]{1,0:T(8,128)}) %reduce-scatter.31.cloned.1.call-update) | async-done | bytes 165904 | tf_op jit(solution)/shard_map/reduce_scatter | solution.py:328
  (416 shorter events, 195.6 us)
Async XLA Ops:
  7.2 85.3 %copy-start.90 = (bf16[288]{0:T(512)(128)(2,1)S(1)}, bf16[288]{0:T(512)(128)(2,1)}, u32[]{:S(2)}) copy-start(bf16[288]{0:T(512)(128)(2,1)} %param.24) | copy-start | bytes 1732
  7.2 117.5 %copy-start.89 = (s32[2]{0:T(128)S(1)}, s32[2]{0:T(128)}, u32[]{:S(2)}) copy-start(s32[2]{0:T(128)} %param.20) | copy-start | bytes 28
  7.2 118.8 %copy-start.56 = (bf16[144,288]{1,0:T(8,128)(2,1)S(1)}, bf16[144,288]{1,0:T(8,128)(2,1)}, u32[]{:S(2)}) copy-start(bf16[144,288]{1,0:T(8,128)(2,1)} %param.26) | copy-start | bytes 248836
  7.2 185.3 %all-gather.19.cloned.1.call-start = ((), (), s32[]{:S(2)}) async-start(), calls=%async_computation.18 | async-start | bytes 2119680 | tf_op jit(solution)/shard_map/all_gather | solution.py:108
  54.6 106.0 %copy-start.91 = (bf16[288]{0:T(512)(128)(2,1)S(1)}, bf16[288]{0:T(512)(128)(2,1)}, u32[]{:S(2)}) copy-start(bf16[288]{0:T(512)(128)(2,1)} %param.27) | copy-start | bytes 1732
  54.6 106.0 %copy-start.57 = (bf16[288,144]{0,1:T(8,128)(2,1)S(1)}, bf16[288,144]{0,1:T(8,128)(2,1)}, u32[]{:S(2)}) copy-start(bf16[288,144]{0,1:T(8,128)(2,1)} %param.28) | copy-start | bytes 248836
  59.2 151.7 %all-gather.11.cloned.1.call-start = ((), (), s32[]{:S(2)}) async-start(), calls=%async_computation.14 | async-start | bytes 2119680 | tf_op jit(solution)/shard_map/all_gather | solution.py:108
  60.0 187.1 %reduce-scatter.47.cloned.1.call-start = ((), (), s32[]{:S(2)}) async-start(), calls=%async_computation.32 | async-start | bytes 4239360
  124.7 86.2 %copy-start.11 = (bf16[1152,288]{1,0:T(8,128)(2,1)}, bf16[1152,288]{1,0:T(8,128)(2,1)S(1)}, u32[]{:S(2)}) copy-start(bf16[1152,288]{1,0:T(8,128)(2,1)S(1)} %all_gather.45) | copy-start | bytes 1990660
  209.9 79.2 %reduce-scatter.43.cloned.1.call-start = ((), (), s32[]{:S(2)}) async-start(), calls=%async_computation.30 | async-start | bytes 4239360
  227.9 83.6 %all-gather.23.cloned.1.call-start = ((), (), s32[]{:S(2)}) async-start(), calls=%async_computation.20 | async-start | bytes 2119680 | tf_op jit(solution)/shard_map/all_gather | solution.py:194
  230.5 138.0 %all-gather.17.cloned.1.call-start = ((), (), s32[]{:S(2)}) async-start(), calls=%async_computation.17 | async-start | bytes 2985984 | tf_op jit(solution)/shard_map/all_gather | solution.py:87
  231.1 193.3 %all-gather.15.cloned.1.call-start = ((), (), s32[]{:S(2)}) async-start(), calls=%async_computation.16 | async-start | bytes 2985984 | tf_op jit(solution)/shard_map/all_gather | solution.py:86
  231.8 213.0 %all-gather.13.cloned.1.call-start = ((), (), s32[]{:S(2)}) async-start(), calls=%async_computation.15 | async-start | bytes 2119680 | tf_op jit(solution)/shard_map/all_gather | solution.py:129
  292.7 174.2 %all-gather.27.cloned.1.call-start = ((), (), s32[]{:S(2)}) async-start(), calls=%async_computation.22 | async-start | bytes 2119680 | tf_op jit(solution)/shard_map/all_gather | solution.py:194
  293.4 195.2 %all-gather.21.cloned.1.call-start = ((), (), s32[]{:S(2)}) async-start(), calls=%async_computation.19 | async-start | bytes 2119680 | tf_op jit(solution)/shard_map/all_gather | solution.py:129
  294.0 236.7 %reduce-scatter.51.cloned.1.call-start = ((), (), s32[]{:S(2)}) async-start(), calls=%async_computation.34 | async-start | bytes 4239360
  460.9 111.8 %reduce-scatter.55.cloned.1.call-start = ((), (), s32[]{:S(2)}) async-start(), calls=%async_computation.36 | async-start | bytes 4239360
  504.4 110.4 %reduce-scatter.45.cloned.1.call-start = ((), (), s32[]{:S(2)}) async-start(), calls=%async_computation.31 | async-start | bytes 4239360
  512.5 144.4 %reduce-scatter.49.cloned.1.call-start = ((), (), s32[]{:S(2)}) async-start(), calls=%async_computation.33 | async-start | bytes 4239360
  520.2 164.7 %all-gather.29.cloned.1.call-start = ((), (), s32[]{:S(2)}) async-start(), calls=%async_computation.23 | async-start | bytes 2119680 | tf_op jit(solution)/shard_map/all_gather | solution.py:213
  574.8 86.5 %copy-start.72 = (f32[184]{0:T(256)S(1)}, f32[184]{0:T(256)}, u32[]{:S(2)}) copy-start(f32[184]{0:T(256)} %copy-done.71) | copy-start | bytes 2212
  574.8 86.5 %copy-start.74 = (f32[184]{0:T(256)S(1)}, f32[184]{0:T(256)}, u32[]{:S(2)}) copy-start(f32[184]{0:T(256)} %copy-done.73) | copy-start | bytes 2212
  664.4 45.7 %all-gather.25.cloned.1.call-start = ((), (), s32[]{:S(2)}) async-start(), calls=%async_computation.21 | async-start | bytes 2119680 | tf_op jit(solution)/shard_map/all_gather | solution.py:213
  665.0 117.2 %reduce-scatter.57.cloned.1.call-start = ((), (), s32[]{:S(2)}) async-start(), calls=%async_computation.37 | async-start | bytes 4239360
  709.8 81.7 %reduce-scatter.53.cloned.1.call-start = ((), (), s32[]{:S(2)}) async-start(), calls=%async_computation.35 | async-start | bytes 4239360
  734.7 167.2 %reduce-scatter.39.cloned.1.call-start = ((), (), s32[]{:S(2)}) async-start(), calls=%async_computation.28 | async-start | bytes 5971968 | tf_op jit(solution)/shard_map/reduce_scatter | solution.py:332
  745.5 264.8 %reduce-scatter.41.cloned.1.call-start = ((), (), s32[]{:S(2)}) async-start(), calls=%async_computation.29 | async-start | bytes 5971968 | tf_op jit(solution)/shard_map/reduce_scatter | solution.py:333
  756.9 323.5 %reduce-scatter.37.cloned.1.call-start = ((), (), s32[]{:S(2)}) async-start(), calls=%async_computation.27 | async-start | bytes 1990656 | tf_op jit(solution)/shard_map/reduce_scatter | solution.py:331
  763.1 386.7 %reduce-scatter.35.cloned.1.call-start = ((), (), s32[]{:S(2)}) async-start(), calls=%async_computation.26 | async-start | bytes 1990656 | tf_op jit(solution)/shard_map/reduce_scatter | solution.py:330
  768.3 450.8 %reduce-scatter.33.cloned.1.call-start = ((), (), s32[]{:S(2)}) async-start(), calls=%async_computation.25 | async-start | bytes 1990656 | tf_op jit(solution)/shard_map/reduce_scatter | solution.py:329
  773.6 514.9 %reduce-scatter.31.cloned.1.call-start = ((), (), s32[]{:S(2)}) async-start(), calls=%async_computation.24 | async-start | bytes 1990656 | tf_op jit(solution)/shard_map/reduce_scatter | solution.py:328
  (105 other events, 985.4 us)
Sparse Core Ops, SparseCore 0:
  59.3 17.5 all-gather.18
  79.1 20.3 all-gather.10
  210.0 36.9 reduce-scatter.46
  249.6 39.4 reduce-scatter.42
  291.1 20.3 all-gather.22
  313.5 55.0 all-gather.16
  370.7 53.5 all-gather.14
  425.9 18.9 all-gather.12
  446.4 20.3 all-gather.26
  468.2 20.3 all-gather.20
  491.1 39.4 reduce-scatter.50
  533.2 39.4 reduce-scatter.54
  575.2 39.4 reduce-scatter.44
  617.3 39.4 reduce-scatter.48
  664.5 20.3 all-gather.28
  686.3 20.3 all-gather.24
  709.9 39.4 reduce-scatter.56
  752.0 39.4 reduce-scatter.52
  795.7 106.1 reduce-scatter.38
  906.4 103.9 reduce-scatter.40
  1014.4 65.8 reduce-scatter.36
  1084.8 64.9 reduce-scatter.34
  1153.8 65.2 reduce-scatter.32
  1223.4 65.0 reduce-scatter.30
